TPU v7x, 32 devices: a whole 2x2x4 slice. The times are simulated.
32 devices in a mesh: tm: 8 (over z, x), pix: 4 (over y, core).
Axes of the slice: x: 2, y: 2, z: 4, core: 2. Of those that a mesh axis runs over, the one named last changes fastest.
Arguments:
- movie: bfloat16 [8, 2048, 2048], P('tm', 'pix'), may hold values from -6 to 6
- shifts: int32 [8, 16, 16, 2], P('tm', 'pix'), may hold values from -16 to 16
- footprints: bfloat16 [4, 256, 64, 4096], P('pix', 'tm'), may hold values from -0.0234375 to 0.0234375
- neuron_ids: int32 [4, 256, 64], P('pix', 'tm'), may hold values from 0 to 4095
Outputs:
- traces: float32 [4096, 8], P(('tm', 'pix'))
All inputs are finite; a program needn't handle non-finite values.
Results may differ from a plain program's by a relative error of at most 0.0029.
Values may be sent and summed in bfloat16 or wider, within the bound.
A program may use at most 128 MiB of HBM per device.

v0:
```python
import jax
import jax.numpy as jnp
from jax import lax
from jax.sharding import PartitionSpec as P

TILE = 128
MAXSHIFT = 16
PATCH = 64
NEURONS = 4096


pixel_sigma = 3.0
frame_sigma = 4.0


def padded_2(shard, sides, width):
    for axis, dim in sides:
        count, length = (lax.axis_size(axis), shard.shape[dim])
        up = [(i, (i + 1) % count) for i in range(count - 1)]
        down = [(j, i) for i, j in up]
        last = lax.slice_in_dim(shard, length - width, length, axis=dim)
        initial = lax.slice_in_dim(shard, 0, width, axis=dim)
        before = lax.ppermute(last, axis, up)
        after = lax.ppermute(initial, axis, down)
        shard = jnp.concatenate([before, shard, after], axis=dim)
    return shard


def gauss_table(count, sigma):
    places = jnp.arange(count).astype(jnp.float32)
    apart = places[:, None] - places[None, :]
    weights = jnp.exp(-apart * apart / (2.0 * sigma * sigma))
    return weights / jnp.sum(weights, axis=1, keepdims=True)


def apply_shift(band, shifts):
    padded = jnp.pad(band, ((0, 0), (0, 0), (MAXSHIFT, MAXSHIFT)))
    frames_dev, rows_pad, cols_pad = padded.shape
    rows_dev = rows_pad - 2 * MAXSHIFT
    width = cols_pad - 2 * MAXSHIFT
    tiles_down = rows_dev // TILE
    tiles_across = width // TILE
    reach = TILE + 2 * MAXSHIFT
    main_rows = padded[:, :rows_dev].reshape(frames_dev, tiles_down, TILE, cols_pad)
    tail_rows = padded[:, rows_dev:][:, None]
    next_rows = jnp.concatenate([main_rows[:, 1:, : 2 * MAXSHIFT], tail_rows], axis=1)
    strips = jnp.concatenate([main_rows, next_rows], axis=2)
    main_cols = strips[..., :width].reshape(frames_dev, tiles_down, reach, tiles_across, TILE)
    tail_cols = strips[..., width:][:, :, :, None, :]
    next_cols = jnp.concatenate([main_cols[:, :, :, 1:, : 2 * MAXSHIFT], tail_cols], axis=3)
    windows = jnp.concatenate([main_cols, next_cols], axis=4)
    vertical = shifts[..., 0]
    horizontal = shifts[..., 1]
    inner = jnp.arange(TILE, dtype=jnp.int32)
    outer = jnp.arange(reach, dtype=jnp.int32)
    pick_rows = (
        outer[None, None, None, None, :]
        == inner[None, None, None, :, None] + MAXSHIFT + vertical[..., None, None]
    ).astype(jnp.bfloat16)
    pick_cols = (
        outer[None, None, None, None, :]
        == inner[None, None, None, :, None] + MAXSHIFT + horizontal[..., None, None]
    ).astype(jnp.bfloat16)
    moved_rows = jnp.einsum(
        "fabij,fajbk->faibk", pick_rows, windows, preferred_element_type=jnp.float32
    ).astype(jnp.bfloat16)
    result = jnp.einsum(
        "faibk,fabxk->faibx", moved_rows, pick_cols, preferred_element_type=jnp.float32
    ).astype(jnp.bfloat16)
    return result.reshape(frames_dev, rows_dev, width)


def highpass(moved):
    frames_all = moved.shape[0]
    side = moved.shape[3]
    base = gauss_table(side, pixel_sigma)
    row_table = base.astype(jnp.bfloat16)
    col_table = jnp.kron(jnp.eye(2, dtype=jnp.float32), base).astype(jnp.bfloat16)
    time_table = gauss_table(frames_all, frame_sigma).astype(jnp.bfloat16)
    along_rows = jnp.einsum(
        "ij,fspjc->fspic", row_table, moved, preferred_element_type=jnp.float32
    ).astype(jnp.bfloat16)
    along_cols = jnp.einsum(
        "fspic,dc->fspid", along_rows, col_table, preferred_element_type=jnp.float32
    ).astype(jnp.bfloat16)
    along_time = jnp.einsum(
        "gf,fspic->gspic", time_table, along_cols, preferred_element_type=jnp.float32
    )
    return (moved.astype(jnp.float32) - along_time).astype(jnp.bfloat16)


def on_device(movie, shifts, footprints, neuron_ids):
    band = padded_2(movie, (("pix", 1),), MAXSHIFT)
    registered = apply_shift(band, shifts)
    frames_dev, rows_dev, width = registered.shape
    side = PATCH
    groups = lax.axis_size("tm")
    arranged = registered.reshape(frames_dev, rows_dev // side, side, width // (2 * side), 2 * side)
    arranged = arranged.transpose(0, 1, 3, 2, 4).reshape(frames_dev, groups, -1, side, 2 * side)
    moved = lax.all_to_all(arranged, "tm", split_axis=1, concat_axis=0, tiled=True)
    cleaned = highpass(moved)
    frames_all = cleaned.shape[0]
    pairs = cleaned.shape[2]
    pixels = cleaned.reshape(frames_all, pairs, side, 2, side)
    blocks = footprints.reshape(pairs, 2, footprints.shape[2], side, side)
    partial_value = jnp.einsum(
        "fpihc,phkic->phkf", pixels, blocks, preferred_element_type=jnp.float32
    )
    partial_value = partial_value.reshape(-1, frames_all)
    labels = neuron_ids.reshape(-1)
    wanted = jnp.arange(
        NEURONS // (groups * lax.axis_size("pix")) * lax.axis_size(("tm", "pix")), dtype=jnp.int32
    )
    onehot = (wanted[:, None] == labels[None, :]).astype(jnp.float32)
    return lax.psum_scatter(
        jnp.dot(
            onehot,
            partial_value,
            precision=lax.Precision.HIGHEST,
            preferred_element_type=jnp.float32,
        ),
        ("tm", "pix"),
        scatter_dimension=0,
        tiled=True,
    )


def solution(mesh):
    in_specs = (
        P("tm", "pix", None),
        P("tm", "pix", None, None),
        P("pix", "tm", None, None),
        P("pix", "tm", None),
    )
    out_specs = P(("tm", "pix"), None)
    return jax.shard_map(
        on_device, mesh=mesh, in_specs=in_specs, out_specs=out_specs, check_vma=False
    )
```

profile of v0, /device:TPU:0, one launch (start us, length us, event | category | flops | bytes accessed | tf_op | source)
XLA Modules:
  0.0 326.2 jit_solution(7241340730157690568)
XLA Ops:
  6.5 0.9 fusion.57
  7.4 2.4 collective-permute-start
  9.8 1.3 collective-permute-start.1
  11.1 0.8 fusion.58
  12.0 3.1 collective-permute-done.1
  15.1 4.1 %fusion.19 = bf16[1,544,2080]{2,1,0:T(8,128)(2,1)S(1)} fusion(bf16[1,16,2048]{2,1,0:T(8,128)(2,1)S(1)} %collective-permute-done.1, bf16[1,512,2048]{2,1,0:T(8,128)(2,1)} %param.4, bf16[1,16,2048]{2,1,0:T(8,128)(2,1)S(1)} %collective-permute-done), kind=kLoop, calls=%fused_computation.28 | loop fusion | flops 13578240 | bytes 4491264 | tf_op jit(solution)/shard_map/concatenate | solution.py:25
  19.2 0.2 slice.40
  19.4 1.3 copy-done.1
  20.7 3.1 copy.33
  23.9 1.8 copy.34
  25.7 2.2 fusion.9
  28.0 1.9 copy-done.2
  30.0 4.9 %convert_bitcast_fusion.1 = bf16[1,4,128,16,128]{4,2,3,1,0:T(8,128)(2,1)S(1)} fusion(s32[4,16,128]{2,1,0:T(8,128)S(1)} %get-tuple-element.10, bf16[1,4,160,1,32]{2,4,3,1,0:T(8,128)(2,1)S(1)} %fusion.34, bf16[1,4,160,15,32]{2,4,3,1,0:T(8,128)(2,1)S(1)} %slice.45, bf16[1,4,160,16,128]{2,4,3,1,0:T(8,128)(2,1)} %bitcast.75, s32[4,16,128]{2,1,0:T(8,128)S(1)} %get-tuple-element.9), kind=kOutput, calls=%fused_computation.36 | convolution fusion | flops 769785856 | bytes 5439488 | tf_op jit(solution)/shard_map/faibk,fabxk->faibx/dot_general | solution.py:67
  34.9 1.4 copy.35
  36.3 1.9 copy.36
  38.1 5.8 %all-to-all-start = ((bf16[1,8,16,64,128]{4,3,2,0,1:T(8,128)(2,1)}), bf16[1,8,16,64,128]{4,3,2,0,1:T(8,128)(2,1)S(1)}, u32[]{:S(2)}, u32[]{:S(2)}) async-start(bf16[1,8,16,64,128]{4,3,2,0,1:T(8,128)(2,1)} %copy.36), calls=%async_computation | async-start | bytes 4194304 | tf_op jit(solution)/shard_map/all_to_all | solution.py:100
  43.9 0.2 reduce-scatter.2.cloned.1.call-start
  44.2 0.2 fusion.40
  44.4 0.1 fusion.39
  44.5 0.1 multiply_convert_fusion
  44.6 0.1 reshape.162
  44.7 46.0 %reshape.159 = bf16[16,2,64,64,64]{4,3,2,1,0:T(8,128)(2,1)} reshape(bf16[1,32,64,4096]{3,2,1,0:T(8,128)(2,1)} %param.6) | data formatting | bytes 33554432 | tf_op jit(solution)/shard_map/reshape | solution.py:105
  90.7 44.4 %copy.40 = bf16[16,2,64,64,64]{3,2,4,1,0:T(8,128)(2,1)} copy(bf16[16,2,64,64,64]{4,3,2,1,0:T(8,128)(2,1)} %reshape.159) | data formatting | bytes 33554432 | tf_op jit(solution)/shard_map/reshape | solution.py:105
  135.2 0.2 fusion.46
  135.4 2.1 convert_bitcast_fusion
  137.4 5.2 %fusion.24 = f32[8,16,64,128]{3,0,2,1:T(8,128)} fusion(bf16[8,16,64,128]{3,2,1,0:T(8,128)(2,1)} %convert_bitcast_fusion, bf16[128,128,1,1]{1,0,2,3:T(8,128)(2,1)S(1)} %reshape.162, f32[8]{0:T(128)S(1)} %fusion.46, f32[8]{0:T(128)S(1)} %iota_convert_fusion.1), kind=kOutput, calls=%fused_computation.33 | convolution fusion | flops 286261632 | bytes 6324288 | tf_op jit(solution)/shard_map/gf,fspic->gspic/dot_general | solution.py:86
  142.6 4.5 %fusion.10 = bf16[8,16,64,128]{3,2,1,0:T(8,128)(2,1)} fusion(f32[8,16,64,128]{3,0,2,1:T(8,128)} %fusion.24, bf16[1,8,16,64,128]{4,3,2,0,1:T(8,128)(2,1)S(1)} %all-to-all-done), kind=kLoop, calls=%fused_computation.19 | loop fusion | flops 3145728 | bytes 8388608 | tf_op jit(solution)/shard_map/convert_element_type | solution.py:89
  147.2 5.0 %copy.46 = bf16[8,16,64,128]{2,0,3,1:T(8,128)(2,1)} copy(bf16[8,16,64,128]{3,2,1,0:T(8,128)(2,1)} %fusion.10) | data formatting | bytes 4194304 | tf_op jit(solution)/shard_map/reshape | solution.py:104
  152.2 15.5 %convolution_bitcast_fusion = f32[16,2,64,8]{2,3,1,0:T(8,128)S(1)} fusion(bf16[8,16,64,2,64]{2,0,4,3,1:T(8,128)(2,1)} %bitcast.70, bf16[16,2,64,64,64]{3,2,4,1,0:T(8,128)(2,1)} %copy.40), kind=kOutput, calls=%fused_computation.37 | convolution fusion | flops 134217728 | bytes 18939904 | tf_op jit(solution)/shard_map/fpihc,phkic->phkf/dot_general | solution.py:106
  167.8 0.2 reshape.160
  168.0 15.3 %fusion = f32[4096,8]{0,1:T(8,128)} fusion(f32[2048,8]{0,1:T(8,128)S(1)} %reshape.160, s32[2048]{0:T(1024)S(1)} %eq.55), kind=kOutput, calls=%fused_computation.1 | convolution fusion | flops 813694976 | bytes 204800 | tf_op jit(solution)/shard_map/dot_general | solution.py:116
  183.3 136.0 %reduce-scatter.2.cloned.1.call-done = f32[128,8]{0,1:T(8,128)} async-done(((f32[4096,8]{0,1:T(8,128)}), f32[128,8]{0,1:T(8,128)}) %reduce-scatter.2.cloned.1.call-update) | async-done | bytes 4112 | tf_op jit(solution)/shard_map/reduce_scatter | solution.py:115
  (21 shorter events, 0.5 us)
Async XLA Ops:
  7.4 4.5 %collective-permute-start = (bf16[1,16,2048]{2,1,0:T(8,128)(2,1)S(1)}, bf16[1,16,2048]{2,1,0:T(8,128)(2,1)S(1)}, u32[]{:S(2)}, u32[]{:S(2)}) collective-permute-start(bf16[1,16,2048]{2,1,0:T(8,128)(2,1)S(1)} %get-tuple-element.5), channel_id=1, source_target_pairs={{0,1},{1,2},{2,3},{4,5},{5,6},{6,7},{8,9},{9,10},{10,11},{12,13},{... | collective-permute-start | bytes 196616 | tf_op jit(solution)/shard_map/ppermute | solution.py:23
  9.8 5.3 %collective-permute-start.1 = (bf16[1,16,2048]{2,1,0:T(8,128)(2,1)S(1)}, bf16[1,16,2048]{2,1,0:T(8,128)(2,1)S(1)}, u32[]{:S(2)}, u32[]{:S(2)}) collective-permute-start(bf16[1,16,2048]{2,1,0:T(8,128)(2,1)S(1)} %get-tuple-element.6), channel_id=1, source_target_pairs={{1,0},{2,1},{3,2},{5,4},{6,5},{7,6},{9,8},{10,9},{11,10},{13,12},{... | collective-permute-start | bytes 196616 | tf_op jit(solution)/shard_map/ppermute | solution.py:24
  19.3 1.4 copy-start.1
  25.7 2.2 copy-start
  28.0 1.9 copy-start.2
  38.1 97.2 %all-to-all-start = ((bf16[1,8,16,64,128]{4,3,2,0,1:T(8,128)(2,1)}), bf16[1,8,16,64,128]{4,3,2,0,1:T(8,128)(2,1)S(1)}, u32[]{:S(2)}, u32[]{:S(2)}) async-start(bf16[1,8,16,64,128]{4,3,2,0,1:T(8,128)(2,1)} %copy.36), calls=%async_computation | async-start | bytes 4194304 | tf_op jit(solution)/shard_map/all_to_all | solution.py:100
  43.9 275.4 %reduce-scatter.2.cloned.1.call-start = ((), (), s32[]{:S(2)}) async-start(), calls=%async_computation.2 | async-start | bytes 135168 | tf_op jit(solution)/shard_map/reduce_scatter | solution.py:115
  90.7 44.4 %copy-start.3 = (s32[1,32,64]{2,1,0:T(8,128)S(1)}, s32[1,32,64]{2,1,0:T(8,128)}, u32[]{:S(2)}) copy-start(s32[1,32,64]{2,1,0:T(8,128)} %param.7) | copy-start | bytes 24580
Sparse Core Ops, SparseCore 0:
  183.4 135.8 reduce-scatter.1
where the time goes:
time: 329 us; the launch traced here: 326 us
  waiting for transfers between devices  139 us (42%)
  local copies, waits for them, and re-layouts  109 us (33%)
  matrix products  43 us (13%)
  between operations  13.6 us (4%)
  other arithmetic  11.6 us (4%)
  starting transfers between devices  9.68 us (3%)
    reduce_scatter x1, waiting for transfers between devices, on_device(): lax.psum_scatter(jnp.dot(onehot, partial_value, precision=lax.Precision.H...  136 us
    reshape x2, local copies, waits for them, and re-layouts, on_device(): blocks = footprints.reshape(pairs, 2, footprints.shape[2], side, side)  90.4 us
    dot_general x1, matrix products, on_device(): jnp.einsum('fpihc,phkic->phkf', pixels, blocks, preferred_element_type=jn...  15.5 us
    dot_general x1, matrix products, on_device(): jnp.dot(onehot, partial_value, precision=lax.Precision.HIGHEST, preferred...  15.3 us
  transfers between devices with their start and end apart: 4, of which 2 were waited for; matrix products, arithmetic and copies ran while one was open for 28% of the time, Pallas kernels for 0%

commit v1 on v0

v1 whole, which is shorter than its diff:
```python
import jax
import jax.numpy as jnp
import ml_dtypes
import numpy as np
from jax import lax
from jax.experimental import pallas as pl
from jax.experimental.pallas import tpu as pltpu
from jax.sharding import PartitionSpec as P

TILE = 128
MAXSHIFT = 16
PATCH = 64
NEURONS = 4096
LANES = 128
GROUP = 4


pixel_sigma = 3.0
frame_sigma = 4.0


def gauss_table(count, sigma):
    places = np.arange(count).astype(np.float32)
    apart = places[:, None] - places[None, :]
    weights = np.exp(-apart * apart / np.float32(2.0 * sigma * sigma)).astype(np.float32)
    table = weights / np.sum(weights, axis=1, keepdims=True, dtype=np.float32)
    return table.astype(ml_dtypes.bfloat16)


def halo(band):
    count = lax.axis_size("pix")
    up = [(i, i + 1) for i in range(count - 1)]
    down = [(i + 1, i) for i in range(count - 1)]
    before = lax.ppermute(band[-MAXSHIFT:], "pix", up)
    after = lax.ppermute(band[:MAXSHIFT], "pix", down)
    return before, after


def register_kernel(shift_ref, band_ref, before_ref, after_ref, out_ref, padded):
    rows, width = band_ref.shape
    across = width // TILE
    tall = rows + 2 * MAXSHIFT
    for j in (0, across + 1):
        padded[j] = jnp.zeros((tall, TILE), jnp.float32)
    for j in range(across):
        lanes = pl.ds(j * TILE, TILE)
        padded[j + 1, pl.ds(0, MAXSHIFT), :] = before_ref[:, lanes].astype(jnp.float32)
        padded[j + 1, pl.ds(MAXSHIFT, rows), :] = band_ref[:, lanes].astype(jnp.float32)
        padded[j + 1, pl.ds(rows + MAXSHIFT, MAXSHIFT), :] = after_ref[:, lanes].astype(jnp.float32)

    gap = lax.broadcasted_iota(jnp.int32, (2 * TILE, TILE), 0) - lax.broadcasted_iota(
        jnp.int32, (2 * TILE, TILE), 1
    )

    @pl.loop(0, rows // TILE)
    def _(a):
        for b in range(across):
            place = (a * across + b) * 2
            dy = shift_ref[place]
            dx = shift_ref[place + 1]
            left = dx < 0
            start = jnp.where(left, b, b + 1)
            at = pl.ds(a * TILE + MAXSHIFT + dy, TILE)
            window = jnp.concatenate([padded[start, at, :], padded[start + 1, at, :]], axis=1)
            pick = (gap == jnp.where(left, dx + TILE, dx)).astype(jnp.float32).astype(jnp.bfloat16)
            moved = jnp.dot(window.astype(jnp.bfloat16), pick, preferred_element_type=jnp.float32)
            out_ref[pl.ds(pl.multiple_of(a * TILE, TILE), TILE), b * TILE : (b + 1) * TILE] = moved.astype(
                jnp.bfloat16
            )


def register(band, before, after, shifts):
    rows, width = band.shape
    vmem = pl.BlockSpec(memory_space=pltpu.VMEM)
    return pl.pallas_call(
        register_kernel,
        out_shape=jax.ShapeDtypeStruct((rows, width), jnp.bfloat16),
        in_specs=[pl.BlockSpec(memory_space=pltpu.SMEM), vmem, vmem, vmem],
        out_specs=vmem,
        scratch_shapes=[pltpu.VMEM((width // TILE + 2, rows + 2 * MAXSHIFT, TILE), jnp.float32)],
        compiler_params=pltpu.CompilerParams(vmem_limit_bytes=24 << 20),
        name="register",
    )(shifts.reshape(-1), band, before, after)


def project_kernel(local, x_ref, foot_ref, ids_ref, row_ref, col_ref, mix_ref, out_ref):
    frames, side, cols = x_ref.shape
    half = row_ref.shape[0] // frames
    moved = x_ref[...].reshape(frames * side, cols)
    chunk = row_ref.shape[0]
    along_rows = jnp.concatenate(
        [
            jnp.dot(row_ref[...], moved[i : i + chunk], preferred_element_type=jnp.float32)
            for i in range(0, frames * side, chunk)
        ],
        axis=0,
    ).astype(jnp.bfloat16)
    along_cols = jnp.dot(along_rows, col_ref[...], preferred_element_type=jnp.float32).astype(jnp.bfloat16)
    patches = cols // side
    low = lax.broadcasted_iota(jnp.int32, (frames, LANES), 1) < side
    pieces = [[] for _ in range(patches)]
    for h in range(side // half):
        stack = [moved[f * side + h * half : f * side + (h + 1) * half] for f in range(frames)]
        stack += [along_cols[f * side + h * half : f * side + (h + 1) * half] for f in range(frames)]
        clean = jnp.dot(mix_ref[...], jnp.concatenate(stack, axis=0), preferred_element_type=jnp.float32)
        for i in range(half // 2):
            for j in range(cols // LANES):
                first = clean[2 * i * frames : (2 * i + 1) * frames, j * LANES : (j + 1) * LANES]
                second = clean[(2 * i + 1) * frames : (2 * i + 2) * frames, j * LANES : (j + 1) * LANES]
                pieces[2 * j].append(jnp.where(low, first, pltpu.roll(second, side, 1)))
                pieces[2 * j + 1].append(jnp.where(low, pltpu.roll(first, side, 1), second))
    pixels = jnp.concatenate([jnp.concatenate(p, axis=1) for p in pieces], axis=0).astype(jnp.bfloat16)
    blocks = foot_ref[...].reshape(patches * foot_ref.shape[1], side * side)
    product = lax.dot_general(pixels, blocks, (((1,), (1,)), ((), ())), preferred_element_type=jnp.float32)
    count = product.shape[1]
    owner_patch = lax.broadcasted_iota(jnp.int32, (frames, count), 1) // foot_ref.shape[1]
    partial = jnp.zeros((frames, count), jnp.float32)
    for p in range(patches):
        partial = jnp.where(owner_patch == p, product[p * frames : (p + 1) * frames], partial)
    ids = ids_ref[0]
    owner = jnp.broadcast_to(ids // local, (frames, count))
    within = ids % local
    onehot = (
        (lax.broadcasted_iota(jnp.int32, (local, count), 0) == within).astype(jnp.float32).astype(jnp.bfloat16)
    )
    total = None
    rest = partial
    for _ in range(3):
        piece = rest.astype(jnp.bfloat16).astype(jnp.float32)
        rest = rest - piece
        spread = jnp.concatenate(
            [jnp.where(owner == o, piece, 0.0) for o in range(NEURONS // local)], axis=0
        ).astype(jnp.bfloat16)
        term = lax.dot_general(spread, onehot, (((1,), (1,)), ((), ())), preferred_element_type=jnp.float32)
        total = term if total is None else total + term

    @pl.when(pl.program_id(0) == 0)
    def _():
        out_ref[...] = total

    @pl.when(pl.program_id(0) > 0)
    def _():
        out_ref[...] += total


def project(moved, footprints, labels, owners):
    frames, side, width = moved.shape
    steps = width // (GROUP * side)
    foot_cols = footprints.shape[1]
    local = NEURONS // owners
    base = gauss_table(side, pixel_sigma)
    time = gauss_table(frames, frame_sigma)
    full = GROUP * side
    eye = np.eye(GROUP, dtype=np.float32)
    row_table = np.kron(eye, base.astype(np.float32)).astype(ml_dtypes.bfloat16)
    col_table = np.kron(eye, base.astype(np.float32).T).astype(ml_dtypes.bfloat16)
    half = full // frames
    spots = np.eye(half, dtype=np.float32)
    keep = np.einsum("gf,rs->rgfs", np.eye(frames, dtype=np.float32), spots)
    blur = np.einsum("gf,rs->rgfs", time.astype(np.float32), spots)
    mix = np.concatenate([keep.reshape(full, full), -blur.reshape(full, full)], axis=1).astype(ml_dtypes.bfloat16)
    fixed = lambda shape: pl.BlockSpec(shape, lambda s: (0,) * len(shape))
    return pl.pallas_call(
        lambda *refs: project_kernel(local, *refs),
        out_shape=jax.ShapeDtypeStruct((owners * frames, local), jnp.float32),
        grid=(steps,),
        in_specs=[
            pl.BlockSpec((frames, side, full), lambda s: (0, 0, s)),
            pl.BlockSpec((GROUP, foot_cols, side * side), lambda s: (s, 0, 0)),
            pl.BlockSpec((1, 1, GROUP * foot_cols), lambda s: (s, 0, 0)),
            fixed(row_table.shape),
            fixed(col_table.shape),
            fixed(mix.shape),
        ],
        out_specs=fixed((owners * frames, local)),
        compiler_params=pltpu.CompilerParams(vmem_limit_bytes=40 << 20),
        name="project",
    )(
        moved,
        footprints,
        labels.reshape(steps, 1, GROUP * foot_cols),
        jnp.asarray(row_table),
        jnp.asarray(col_table),
        jnp.asarray(mix),
    )


def project_general(moved, footprints, labels, owners):
    frames, side, width = moved.shape
    base = jnp.asarray(gauss_table(side, pixel_sigma))
    time = jnp.asarray(gauss_table(frames, frame_sigma))
    blocks = moved.reshape(frames, side, width // side, side)
    dot = lambda spec, a, b: jnp.einsum(spec, a, b, preferred_element_type=jnp.float32)
    along_rows = dot("ij,fjpc->fipc", base, blocks).astype(jnp.bfloat16)
    along_cols = dot("fipc,dc->fipd", along_rows, base).astype(jnp.bfloat16)
    clean = (blocks.astype(jnp.float32) - dot("gf,fipc->gipc", time, along_cols)).astype(jnp.bfloat16)
    pixels = clean.transpose(2, 0, 1, 3).reshape(width // side, frames, side * side)
    partial = dot("pfx,pkx->fpk", pixels, footprints).reshape(frames, -1)
    wanted = jnp.arange(NEURONS, dtype=jnp.int32)
    onehot = (labels.reshape(-1)[:, None] == wanted[None, :]).astype(jnp.float32)
    sums = jnp.dot(partial, onehot, precision=lax.Precision.HIGHEST, preferred_element_type=jnp.float32)
    return sums.reshape(frames, owners, -1).transpose(1, 0, 2).reshape(owners * frames, -1)


def on_device(movie, shifts, footprints, neuron_ids):
    band = movie[0]
    before, after = halo(band)
    registered = register(band, before, after, shifts)
    rows, width = registered.shape
    groups = lax.axis_size("tm")
    owners = groups * lax.axis_size("pix")
    wide = footprints.shape[1] * PATCH
    slabs = registered.reshape(rows // PATCH, PATCH, width // wide, wide)
    slabs = slabs.transpose(0, 2, 1, 3).reshape(groups, PATCH, wide)
    moved = lax.all_to_all(slabs, "tm", split_axis=0, concat_axis=0, tiled=True)
    frames = moved.shape[0]
    fits = frames * 32 == GROUP * PATCH and wide % (GROUP * PATCH) == 0 and NEURONS // owners == LANES
    form = project if fits else project_general
    sums = form(moved, footprints[0], neuron_ids[0], owners)
    sums = lax.all_to_all(
        sums.reshape(owners, frames, -1), ("tm", "pix"), split_axis=0, concat_axis=0, tiled=True
    )
    return jnp.sum(sums, axis=0).T


def solution(mesh):
    in_specs = (
        P("tm", "pix", None),
        P("tm", "pix", None, None),
        P("pix", "tm", None, None),
        P("pix", "tm", None),
    )
    out_specs = P(("tm", "pix"), None)
    return jax.shard_map(
        on_device, mesh=mesh, in_specs=in_specs, out_specs=out_specs, check_vma=False
    )
```

time: 329 us -> 98.6 us (0.30)
  local copies, waits for them, and re-layouts: 109 us -> 4.82 us
  waiting for transfers between devices: 139 us -> 51.3 us
  matrix products: 43 us -> 0 us
  Pallas kernels: 0 us -> 19.9 us
  between operations: 13.6 us -> 0.07 us
  blocking collectives: 0 us -> 12 us
  other arithmetic: 11.6 us -> 0.63 us
    reduce_scatter x1 -> x0, waiting for transfers between devices: 136 us -> none  [on_device(): lax.psum_scatter(jnp.dot(onehot, partial_value, precision=lax.Precision.H...]
    reshape x5 -> x1, local copies, waits for them, and re-layouts: 98.7 us -> 0.14 us  [register(): shifts.reshape(-1)]
    all_to_all x1, waiting for transfers between devices: 0.01 us -> 48.3 us  [on_device(): moved = lax.all_to_all(slabs, 'tm', split_axis=0, concat_axis=0, tiled=True)]
    dot_general x5 -> x0, matrix products: 43 us -> none  [the longest x1 15.5 us: on_device(): jnp.einsum('fpihc,phkic->phkf', pixels, blocks, preferred_element_type=jn...]
    pallas_call x0 -> x2, Pallas kernels: none -> 19.9 us  [the longest x1 17.2 us: project(): pl.pallas_call(lambda *refs: project_kernel(local, *refs), out_shape=jax....]
    all_to_all x0 -> x1, blocking collectives: none -> 12 us  [on_device(): lax.all_to_all(sums.reshape(owners, frames, -1), ('tm', 'pix'), split_axi...]
    concatenate x3 -> x0, other arithmetic: 6.37 us -> none  [the longest x1 4.08 us: padded_2(): shard = jnp.concatenate([before, shard, after], axis=dim)]
    convert_element_type x5 -> x0, other arithmetic: 4.64 us -> none  [the longest x1 4.51 us: highpass(): return (moved.astype(jnp.float32) - along_time).astype(jnp.bfloat16)]
  transfers between devices with their start and end apart: 4 -> 3, of which waited for: 2 -> 2; matrix products, arithmetic and copies ran while one was open for 28% -> 1% of each run, Pallas kernels for 0% -> 0%
where the time goes in v1:
time: 98.6 us; the launch traced here: 98.3 us
  waiting for transfers between devices  51.3 us (52%)
  Pallas kernels  19.9 us (20%)
  blocking collectives  12 us (12%)
  starting transfers between devices  9.6 us (10%)
  local copies, waits for them, and re-layouts  4.82 us (5%)
    all_to_all x1, waiting for transfers between devices, on_device(): moved = lax.all_to_all(slabs, 'tm', split_axis=0, concat_axis=0, tiled=True)  48.3 us
    pallas_call x1, Pallas kernels, project(): pl.pallas_call(lambda *refs: project_kernel(local, *refs), out_shape=jax....  17.2 us
    all_to_all x1, blocking collectives, on_device(): lax.all_to_all(sums.reshape(owners, frames, -1), ('tm', 'pix'), split_axi...  12 us
    all_to_all x1, starting transfers between devices, on_device(): moved = lax.all_to_all(slabs, 'tm', split_axis=0, concat_axis=0, tiled=True)  5.95 us
    unnamed x13, local copies, waits for them, and re-layouts  3.73 us
    ppermute x1, waiting for transfers between devices, halo(): after = lax.ppermute(band[:MAXSHIFT], 'pix', down)  3.05 us
    pallas_call x1, Pallas kernels, register(): pl.pallas_call(register_kernel, out_shape=jax.ShapeDtypeStruct((rows, wid...  2.71 us
    ppermute x1, starting transfers between devices, halo(): before = lax.ppermute(band[-MAXSHIFT:], 'pix', up)  2.36 us
  transfers between devices with their start and end apart: 3, of which 2 were waited for; matrix products, arithmetic and copies ran while one was open for 1% of the time, Pallas kernels for 0%

profile of v1, /device:TPU:0, one launch (start us, length us, event | category | flops | bytes accessed | tf_op | source)
XLA Modules:
  0.0 98.3 jit_solution(1438289578409913604)
XLA Ops:
  0.0 0.9 slice_bitcast_fusion
  0.9 2.4 %collective-permute-start = (bf16[16,2048]{1,0:T(8,128)(2,1)S(1)}, bf16[16,2048]{1,0:T(8,128)(2,1)S(1)}, u32[]{:S(2)}, u32[]{:S(2)}) collective-permute-start(bf16[16,2048]{1,0:T(8,128)(2,1)S(1)} %get-tuple-element.6), channel_id=1, source_target_pairs={{0,1},{1,2},{2,3},{4,5},{5,6},{6,7},{8,9},{9,10},{10,11},{12,13},{... | collective-permute-start | bytes 196616 | tf_op jit(solution)/shard_map/ppermute | solution.py:34
  3.3 1.3 %collective-permute-start.1 = (bf16[16,2048]{1,0:T(8,128)(2,1)S(1)}, bf16[16,2048]{1,0:T(8,128)(2,1)S(1)}, u32[]{:S(2)}, u32[]{:S(2)}) collective-permute-start(bf16[16,2048]{1,0:T(8,128)(2,1)S(1)} %get-tuple-element.5), channel_id=1, source_target_pairs={{1,0},{2,1},{3,2},{5,4},{6,5},{7,6},{9,8},{10,9},{11,10},{13,12},{... | collective-permute-start | bytes 196616 | tf_op jit(solution)/shard_map/ppermute | solution.py:35
  4.6 0.8 copy.9
  5.3 0.1 reshape.8.shift_ref
  5.5 0.0 collective-permute-done.before_ref
  5.5 3.0 %collective-permute-done.1.after_ref = bf16[16,2048]{1,0:T(8,128)(2,1)S(1)} collective-permute-done((bf16[16,2048]{1,0:T(8,128)(2,1)S(1)}, bf16[16,2048]{1,0:T(8,128)(2,1)S(1)}, u32[]{:S(2)}, u32[]{:S(2)}) %collective-permute-start.1) | collective-permute-done | bytes 65568 | tf_op jit(solution)/shard_map/ppermute | solution.py:35
  8.5 0.0 copy-start.1
  8.5 1.6 %copy-done.1 = bf16[1,512,2048]{2,1,0:T(8,128)(2,1)S(1)} copy-done((bf16[1,512,2048]{2,1,0:T(8,128)(2,1)S(1)}, bf16[1,512,2048]{2,1,0:T(8,128)(2,1)}, u32[]{:S(2)}) %copy-start.1) | copy-done | bytes 2097176
  10.1 2.7 %register.1 = bf16[512,2048]{1,0:T(8,128)(2,1)S(1)} custom-call(s32[128]{0:T(128)S(1)} %reshape.8.shift_ref, bf16[512,2048]{1,0:T(8,128)(2,1)S(1)} %bitcast.12, bf16[16,2048]{1,0:T(8,128)(2,1)S(1)} %collective-permute-done.before_ref, bf16[16,2048]{1,0:T(8,128)(2,1)S(1)} %collective-permute-done.1.after_ref), custom_call_target="tpu_custom_call" | custom-call | tf_op jit(solution)/shard_map/register/pallas_call | solution.py:75
  12.8 0.0 copy-start
  12.9 1.3 %copy-done = bf16[512,2048]{1,0:T(8,128)(2,1)} copy-done((bf16[512,2048]{1,0:T(8,128)(2,1)}, bf16[512,2048]{1,0:T(8,128)(2,1)S(1)}, u32[]{:S(2)}) %copy-start) | copy-done | bytes 2097176
  14.2 0.0 copy-start.5
  14.2 0.0 copy-start.2
  14.2 0.0 copy-start.3
  14.2 0.0 copy-start.4
  14.2 6.0 %all-to-all-start = ((bf16[8,64,2048]{2,1,0:T(8,128)(2,1)}), bf16[8,64,2048]{2,1,0:T(8,128)(2,1)S(1)}, u32[]{:S(2)}, u32[]{:S(2)}) async-start(bf16[8,64,2048]{2,1,0:T(8,128)(2,1)} %bitcast.11), calls=%async_computation | async-start | bytes 4194304 | tf_op jit(solution)/shard_map/all_to_all | solution.py:215
  20.2 0.0 copy-done.5
  20.2 0.1 reshape_squeeze.3.refs_2_
  20.2 48.3 %all-to-all-done.refs_0_ = bf16[8,64,2048]{2,1,0:T(8,128)(2,1)S(1)} async-done(((bf16[8,64,2048]{2,1,0:T(8,128)(2,1)}), bf16[8,64,2048]{2,1,0:T(8,128)(2,1)S(1)}, u32[]{:S(2)}, u32[]{:S(2)}) %all-to-all-start) | async-done | bytes 2097184 | tf_op jit(solution)/shard_map/all_to_all | solution.py:215
  68.5 0.0 copy-done.2
  68.5 0.0 copy-done.3
  68.5 0.0 copy-done.4
  68.5 17.2 %project.1 = f32[256,128]{1,0:T(8,128)S(1)} custom-call(bf16[8,64,2048]{2,1,0:T(8,128)(2,1)S(1)} %all-to-all-done.refs_0_, bf16[32,64,4096]{2,1,0:T(8,128)(2,1)} %bitcast.14, s32[8,1,256]{2,1,0:T(1,128)S(1)} %reshape_squeeze.3.refs_2_, bf16[256,256]{1,0:T(8,128)(2,1)S(1)} %copy-done.3, bf16[256,256]{1,0:T(8,128)(2,1)S(1)} %copy-done.4, ...), custom_call_target="tpu_custom_call" | custom-call | tf_op jit(solution)/shard_map/project/pallas_call | solution.py:163
  85.7 12.0 %all_to_all.10 = f32[32,8,128]{2,1,0:T(8,128)S(1)} all-to-all(f32[32,8,128]{2,1,0:T(8,128)S(1)} %bitcast.13), channel_id=1, replica_groups=mesh['tm'=8,'pix'=4] {'tm','pix'}, dimensions={0} | all-to-all | bytes 262144 | tf_op jit(solution)/shard_map/all_to_all | solution.py:220
  97.7 0.6 reduce_sum.9
Async XLA Ops:
  0.9 4.6 %collective-permute-start = (bf16[16,2048]{1,0:T(8,128)(2,1)S(1)}, bf16[16,2048]{1,0:T(8,128)(2,1)S(1)}, u32[]{:S(2)}, u32[]{:S(2)}) collective-permute-start(bf16[16,2048]{1,0:T(8,128)(2,1)S(1)} %get-tuple-element.6), channel_id=1, source_target_pairs={{0,1},{1,2},{2,3},{4,5},{5,6},{6,7},{8,9},{9,10},{10,11},{12,13},{... | collective-permute-start | bytes 196616 | tf_op jit(solution)/shard_map/ppermute | solution.py:34
  3.3 5.3 %collective-permute-start.1 = (bf16[16,2048]{1,0:T(8,128)(2,1)S(1)}, bf16[16,2048]{1,0:T(8,128)(2,1)S(1)}, u32[]{:S(2)}, u32[]{:S(2)}) collective-permute-start(bf16[16,2048]{1,0:T(8,128)(2,1)S(1)} %get-tuple-element.5), channel_id=1, source_target_pairs={{1,0},{2,1},{3,2},{5,4},{6,5},{7,6},{9,8},{10,9},{11,10},{13,12},{... | collective-permute-start | bytes 196616 | tf_op jit(solution)/shard_map/ppermute | solution.py:35
  8.5 1.6 %copy-start.1 = (bf16[1,512,2048]{2,1,0:T(8,128)(2,1)S(1)}, bf16[1,512,2048]{2,1,0:T(8,128)(2,1)}, u32[]{:S(2)}) copy-start(bf16[1,512,2048]{2,1,0:T(8,128)(2,1)} %param.7) | copy-start | bytes 6291460
  12.8 1.3 %copy-start = (bf16[512,2048]{1,0:T(8,128)(2,1)}, bf16[512,2048]{1,0:T(8,128)(2,1)S(1)}, u32[]{:S(2)}) copy-start(bf16[512,2048]{1,0:T(8,128)(2,1)S(1)} %register.1) | copy-start | bytes 6291460
  14.2 6.0 %copy-start.5 = (s32[1,32,64]{2,1,0:T(8,128)S(1)}, s32[1,32,64]{2,1,0:T(8,128)}, u32[]{:S(2)}) copy-start(s32[1,32,64]{2,1,0:T(8,128)} %param.10) | copy-start | bytes 24580
  14.2 54.3 %copy-start.2 = (bf16[256,512]{1,0:T(8,128)(2,1)S(1)}, bf16[256,512]{1,0:T(8,128)(2,1)}, u32[]{:S(2)}) copy-start(bf16[256,512]{1,0:T(8,128)(2,1)} %constant.10.clone.refs_5_) | copy-start | bytes 786436
  14.2 54.3 %copy-start.3 = (bf16[256,256]{1,0:T(8,128)(2,1)S(1)}, bf16[256,256]{1,0:T(8,128)(2,1)}, u32[]{:S(2)}) copy-start(bf16[256,256]{1,0:T(8,128)(2,1)} %constant.8.clone.refs_3_) | copy-start | bytes 393220
  14.2 54.3 %copy-start.4 = (bf16[256,256]{1,0:T(8,128)(2,1)S(1)}, bf16[256,256]{1,0:T(8,128)(2,1)}, u32[]{:S(2)}) copy-start(bf16[256,256]{1,0:T(8,128)(2,1)} %constant.9.clone.refs_4_) | copy-start | bytes 393220
  14.2 54.3 %all-to-all-start = ((bf16[8,64,2048]{2,1,0:T(8,128)(2,1)}), bf16[8,64,2048]{2,1,0:T(8,128)(2,1)S(1)}, u32[]{:S(2)}, u32[]{:S(2)}) async-start(bf16[8,64,2048]{2,1,0:T(8,128)(2,1)} %bitcast.11), calls=%async_computation | async-start | bytes 4194304 | tf_op jit(solution)/shard_map/all_to_all | solution.py:215

commit v2 on v1

--- a/solution.py
+++ b/solution.py
@@ -83,10 +83,11 @@
     )(shifts.reshape(-1), band, before, after)
 
 
-def project_kernel(local, x_ref, foot_ref, ids_ref, row_ref, col_ref, mix_ref, out_ref):
-    frames, side, cols = x_ref.shape
+def project_step(local, x, blocks, ids, row_ref, col_ref, mix_ref):
+    frames, side, cols = x.shape
+    foot_cols = blocks.shape[1]
     half = row_ref.shape[0] // frames
-    moved = x_ref[...].reshape(frames * side, cols)
+    moved = x.reshape(frames * side, cols)
     chunk = row_ref.shape[0]
     along_rows = jnp.concatenate(
         [
@@ -110,14 +111,13 @@
                 pieces[2 * j].append(jnp.where(low, first, pltpu.roll(second, side, 1)))
                 pieces[2 * j + 1].append(jnp.where(low, pltpu.roll(first, side, 1), second))
     pixels = jnp.concatenate([jnp.concatenate(p, axis=1) for p in pieces], axis=0).astype(jnp.bfloat16)
-    blocks = foot_ref[...].reshape(patches * foot_ref.shape[1], side * side)
+    blocks = blocks.reshape(patches * foot_cols, side * side)
     product = lax.dot_general(pixels, blocks, (((1,), (1,)), ((), ())), preferred_element_type=jnp.float32)
     count = product.shape[1]
-    owner_patch = lax.broadcasted_iota(jnp.int32, (frames, count), 1) // foot_ref.shape[1]
+    owner_patch = lax.broadcasted_iota(jnp.int32, (frames, count), 1) // foot_cols
     partial = jnp.zeros((frames, count), jnp.float32)
     for p in range(patches):
         partial = jnp.where(owner_patch == p, product[p * frames : (p + 1) * frames], partial)
-    ids = ids_ref[0]
     owner = jnp.broadcast_to(ids // local, (frames, count))
     within = ids % local
     onehot = (
@@ -133,18 +133,132 @@
         ).astype(jnp.bfloat16)
         term = lax.dot_general(spread, onehot, (((1,), (1,)), ((), ())), preferred_element_type=jnp.float32)
         total = term if total is None else total + term
-
-    @pl.when(pl.program_id(0) == 0)
-    def _():
-        out_ref[...] = total
-
-    @pl.when(pl.program_id(0) > 0)
-    def _():
-        out_ref[...] += total
-
-
-def project(moved, footprints, labels, owners):
-    frames, side, width = moved.shape
+    return total
+
+
+def exchange_kernel(
+    local, slab_ref, foot_ref, ids_ref, row_ref, col_ref, mix_ref, out_ref, moved, feet, send, recv, here, feed
+):
+    groups, side, width = slab_ref.shape
+    steps = ids_ref.shape[0]
+    wide = width // steps
+    me = lax.axis_index("tm")
+    barrier = pltpu.get_barrier_semaphore()
+    for d in range(1, groups):
+        pl.semaphore_signal(
+            barrier, inc=1, device_id={"tm": lax.rem(me + d, groups)}, device_id_type=pl.DeviceIdType.MESH
+        )
+    own = pltpu.make_async_copy(slab_ref.at[me], moved.at[me], here)
+    own.start()
+
+    def feet_copy(s):
+        return pltpu.make_async_copy(foot_ref.at[pl.ds(s * GROUP, GROUP)], feet.at[s], feed.at[s])
+
+    def send_copy(s, d):
+        to = lax.rem(me + d, groups)
+        lanes = pl.ds(pl.multiple_of(s * wide, wide), wide)
+        return pltpu.make_async_remote_copy(
+            src_ref=slab_ref.at[to, :, lanes],
+            dst_ref=moved.at[me, :, lanes],
+            send_sem=send.at[s, d - 1],
+            recv_sem=recv.at[s, d - 1],
+            device_id={"tm": to},
+            device_id_type=pl.DeviceIdType.MESH,
+        )
+
+    pl.semaphore_wait(barrier, groups - 1)
+
+    @pl.loop(0, steps)
+    def _(s):
+        for d in range(1, groups):
+            send_copy(s, d).start()
+
+    @pl.loop(0, steps)
+    def _(s):
+        feet_copy(s).start()
+
+    out_ref[...] = jnp.zeros_like(out_ref)
+    own.wait()
+
+    @pl.loop(0, steps)
+    def _(s):
+        feet_copy(s).wait()
+        for d in range(1, groups):
+            send_copy(s, d).wait_recv()
+        lanes = pl.ds(pl.multiple_of(s * wide, wide), wide)
+        out_ref[...] += project_step(local, moved[:, :, lanes], feet[s], ids_ref[s], row_ref, col_ref, mix_ref)
+
+    @pl.loop(0, steps)
+    def _(s):
+        for d in range(1, groups):
+            send_copy(s, d).wait_send()
+
+
+def collect_kernel(sums_ref, out_ref, landed, send, recv):
+    owners = sums_ref.shape[0]
+    across = lax.axis_size("pix")
+    me = lax.axis_index("tm") * across + lax.axis_index("pix")
+    barrier = pltpu.get_barrier_semaphore()
+
+    def place(t):
+        return {"tm": t // across, "pix": lax.rem(t, across)}
+
+    @pl.loop(1, owners)
+    def _(d):
+        pl.semaphore_signal(
+            barrier, inc=1, device_id=place(lax.rem(me + d, owners)), device_id_type=pl.DeviceIdType.MESH
+        )
+
+    pl.semaphore_wait(barrier, owners - 1)
+
+    def copy(d):
+        to = lax.rem(me + d, owners)
+        return pltpu.make_async_remote_copy(
+            src_ref=sums_ref.at[to],
+            dst_ref=landed.at[me],
+            send_sem=send.at[d - 1],
+            recv_sem=recv.at[d - 1],
+            device_id=place(to),
+            device_id_type=pl.DeviceIdType.MESH,
+        )
+
+    @pl.loop(1, owners)
+    def _(d):
+        copy(d).start()
+
+    landed[me] = sums_ref[me]
+
+    @pl.loop(1, owners)
+    def _(d):
+        copy(d).wait_recv()
+
+    out_ref[...] = jnp.sum(landed[...], axis=0)
+
+    @pl.loop(1, owners)
+    def _(d):
+        copy(d).wait_send()
+
+
+def collect(sums):
+    owners, frames, local = sums.shape
+    vmem = pl.BlockSpec(memory_space=pltpu.VMEM)
+    return pl.pallas_call(
+        collect_kernel,
+        out_shape=jax.ShapeDtypeStruct((frames, local), jnp.float32),
+        in_specs=[vmem],
+        out_specs=vmem,
+        scratch_shapes=[
+            pltpu.VMEM((owners, frames, local), jnp.float32),
+            pltpu.SemaphoreType.DMA((owners - 1,)),
+            pltpu.SemaphoreType.DMA((owners - 1,)),
+        ],
+        compiler_params=pltpu.CompilerParams(collective_id=1, has_side_effects=True),
+        name="collect",
+    )(sums)
+
+
+def exchange_project(slabs, footprints, labels, owners):
+    frames, side, width = slabs.shape
     steps = width // (GROUP * side)
     foot_cols = footprints.shape[1]
     local = NEURONS // owners
@@ -159,24 +273,26 @@
     keep = np.einsum("gf,rs->rgfs", np.eye(frames, dtype=np.float32), spots)
     blur = np.einsum("gf,rs->rgfs", time.astype(np.float32), spots)
     mix = np.concatenate([keep.reshape(full, full), -blur.reshape(full, full)], axis=1).astype(ml_dtypes.bfloat16)
-    fixed = lambda shape: pl.BlockSpec(shape, lambda s: (0,) * len(shape))
+    vmem = pl.BlockSpec(memory_space=pltpu.VMEM)
     return pl.pallas_call(
-        lambda *refs: project_kernel(local, *refs),
+        lambda *refs: exchange_kernel(local, *refs),
         out_shape=jax.ShapeDtypeStruct((owners * frames, local), jnp.float32),
-        grid=(steps,),
-        in_specs=[
-            pl.BlockSpec((frames, side, full), lambda s: (0, 0, s)),
-            pl.BlockSpec((GROUP, foot_cols, side * side), lambda s: (s, 0, 0)),
-            pl.BlockSpec((1, 1, GROUP * foot_cols), lambda s: (s, 0, 0)),
-            fixed(row_table.shape),
-            fixed(col_table.shape),
-            fixed(mix.shape),
+        in_specs=[vmem, pl.BlockSpec(memory_space=pl.ANY), vmem, vmem, vmem, vmem],
+        out_specs=vmem,
+        scratch_shapes=[
+            pltpu.VMEM((frames, side, width), jnp.bfloat16),
+            pltpu.VMEM((steps, GROUP, foot_cols, side * side), jnp.bfloat16),
+            pltpu.SemaphoreType.DMA((steps, frames - 1)),
+            pltpu.SemaphoreType.DMA((steps, frames - 1)),
+            pltpu.SemaphoreType.DMA,
+            pltpu.SemaphoreType.DMA((steps,)),
         ],
-        out_specs=fixed((owners * frames, local)),
-        compiler_params=pltpu.CompilerParams(vmem_limit_bytes=40 << 20),
-        name="project",
+        compiler_params=pltpu.CompilerParams(
+            vmem_limit_bytes=44 << 20, collective_id=0, has_side_effects=True
+        ),
+        name="exchange_project",
     )(
-        moved,
+        slabs,
         footprints,
         labels.reshape(steps, 1, GROUP * foot_cols),
         jnp.asarray(row_table),
@@ -212,11 +328,13 @@
     wide = footprints.shape[1] * PATCH
     slabs = registered.reshape(rows // PATCH, PATCH, width // wide, wide)
     slabs = slabs.transpose(0, 2, 1, 3).reshape(groups, PATCH, wide)
+    frames = groups * movie.shape[0]
+    fits = frames * 32 == GROUP * PATCH and wide % (GROUP * PATCH) == 0 and NEURONS // owners == LANES
+    if fits:
+        sums = exchange_project(slabs, footprints[0], neuron_ids[0], owners)
+        return collect(sums.reshape(owners, frames, -1)).T
     moved = lax.all_to_all(slabs, "tm", split_axis=0, concat_axis=0, tiled=True)
-    frames = moved.shape[0]
-    fits = frames * 32 == GROUP * PATCH and wide % (GROUP * PATCH) == 0 and NEURONS // owners == LANES
-    form = project if fits else project_general
-    sums = form(moved, footprints[0], neuron_ids[0], owners)
+    sums = project_general(moved, footprints[0], neuron_ids[0], owners)
     sums = lax.all_to_all(
         sums.reshape(owners, frames, -1), ("tm", "pix"), split_axis=0, concat_axis=0, tiled=True
     )

time: 98.6 us -> 79.5 us (0.81)
  waiting for transfers between devices: 51.3 us -> 2.25 us
  Pallas kernels: 19.9 us -> 67.1 us
  blocking collectives: 12 us -> 0 us
  starting transfers between devices: 9.6 us -> 3.65 us
  local copies, waits for them, and re-layouts: 4.82 us -> 6.12 us
    all_to_all x1 -> x0, waiting for transfers between devices: 48.3 us -> none  [on_device(): moved = lax.all_to_all(slabs, 'tm', split_axis=0, concat_axis=0, tiled=True)]
    pallas_call x1 -> x2, Pallas kernels: 17.2 us -> 64.3 us  [the longest x1 52 us: exchange_project(): pl.pallas_call(lambda *refs: exchange_kernel(local, *refs), out_shape=jax...]
    all_to_all x1 -> x0, blocking collectives: 12 us -> none  [on_device(): lax.all_to_all(sums.reshape(owners, frames, -1), ('tm', 'pix'), split_axi...]
    all_to_all x1 -> x0, starting transfers between devices: 5.95 us -> none  [on_device(): moved = lax.all_to_all(slabs, 'tm', split_axis=0, concat_axis=0, tiled=True)]
    unnamed x13 -> x12, local copies, waits for them, and re-layouts: 3.73 us -> 4.3 us
  transfers between devices with their start and end apart: 3 -> 2, of which waited for: 2 -> 1; matrix products, arithmetic and copies ran while one was open for 1% -> 2% of each run, Pallas kernels for 0% -> 0%
where the time goes in v2:
time: 79.5 us; the launch traced here: 79.2 us
  Pallas kernels  67.1 us (84%)
  local copies, waits for them, and re-layouts  6.12 us (8%)
  starting transfers between devices  3.65 us (5%)
  waiting for transfers between devices  2.25 us (3%)
    pallas_call x1, Pallas kernels, exchange_project(): pl.pallas_call(lambda *refs: exchange_kernel(local, *refs), out_shape=jax...  52 us
    pallas_call x1, Pallas kernels, collect(): pl.pallas_call(collect_kernel, out_shape=jax.ShapeDtypeStruct((frames, lo...  12.4 us
    unnamed x12, local copies, waits for them, and re-layouts  4.3 us
    pallas_call x1, Pallas kernels, register(): pl.pallas_call(register_kernel, out_shape=jax.ShapeDtypeStruct((rows, wid...  2.72 us
    ppermute x1, starting transfers between devices, halo(): before = lax.ppermute(band[-MAXSHIFT:], 'pix', up)  2.36 us
    ppermute x1, waiting for transfers between devices, halo(): after = lax.ppermute(band[:MAXSHIFT], 'pix', down)  2.25 us
  transfers between devices with their start and end apart: 2, of which 1 were waited for; matrix products, arithmetic and copies ran while one was open for 2% of the time, Pallas kernels for 0%

profile of v2, /device:TPU:0, one launch (start us, length us, event | category | flops | bytes accessed | tf_op | source)
XLA Modules:
  0.0 79.2 jit_solution(4323463730080528757)
XLA Ops:
  0.0 0.9 %slice_bitcast_fusion = (bf16[16,2048]{1,0:T(8,128)(2,1)S(1)}, bf16[16,2048]{1,0:T(8,128)(2,1)S(1)}) fusion(bf16[1,512,2048]{2,1,0:T(8,128)(2,1)} %param.7), kind=kLoop, calls=%fused_computation | loop fusion | bytes 262144 | tf_op jit(solution)/shard_map/slice | solution.py:35
  0.9 2.4 %collective-permute-start = (bf16[16,2048]{1,0:T(8,128)(2,1)S(1)}, bf16[16,2048]{1,0:T(8,128)(2,1)S(1)}, u32[]{:S(2)}, u32[]{:S(2)}) collective-permute-start(bf16[16,2048]{1,0:T(8,128)(2,1)S(1)} %get-tuple-element.6), channel_id=1, source_target_pairs={{0,1},{1,2},{2,3},{4,5},{5,6},{6,7},{8,9},{9,10},{10,11},{12,13},{... | collective-permute-start | bytes 196616 | tf_op jit(solution)/shard_map/ppermute | solution.py:34
  3.3 1.3 %collective-permute-start.1 = (bf16[16,2048]{1,0:T(8,128)(2,1)S(1)}, bf16[16,2048]{1,0:T(8,128)(2,1)S(1)}, u32[]{:S(2)}, u32[]{:S(2)}) collective-permute-start(bf16[16,2048]{1,0:T(8,128)(2,1)S(1)} %get-tuple-element.5), channel_id=1, source_target_pairs={{1,0},{2,1},{3,2},{5,4},{6,5},{7,6},{9,8},{10,9},{11,10},{13,12},{... | collective-permute-start | bytes 196616 | tf_op jit(solution)/shard_map/ppermute | solution.py:35
  4.6 0.8 copy.9
  5.3 0.1 reshape.8.shift_ref
  5.5 0.8 %reshape_squeeze.3.refs_2_ = s32[8,1,256]{2,1,0:T(1,128)S(1)} reshape(s32[1,32,64]{2,1,0:T(8,128)} %param.10) | data formatting | bytes 16384 | tf_op jit(solution)/shard_map/reshape;squeeze | solution.py:297
  6.3 0.0 collective-permute-done.before_ref
  6.3 2.3 %collective-permute-done.1.after_ref = bf16[16,2048]{1,0:T(8,128)(2,1)S(1)} collective-permute-done((bf16[16,2048]{1,0:T(8,128)(2,1)S(1)}, bf16[16,2048]{1,0:T(8,128)(2,1)S(1)}, u32[]{:S(2)}, u32[]{:S(2)}) %collective-permute-start.1) | collective-permute-done | bytes 65568 | tf_op jit(solution)/shard_map/ppermute | solution.py:35
  8.5 0.0 copy-start
  8.5 1.6 %copy-done = bf16[1,512,2048]{2,1,0:T(8,128)(2,1)S(1)} copy-done((bf16[1,512,2048]{2,1,0:T(8,128)(2,1)S(1)}, bf16[1,512,2048]{2,1,0:T(8,128)(2,1)}, u32[]{:S(2)}) %copy-start) | copy-done | bytes 2097176
  10.1 0.0 copy-start.2
  10.1 0.0 copy-start.3
  10.1 0.0 copy-start.4
  10.1 2.7 %register.1 = bf16[512,2048]{1,0:T(8,128)(2,1)S(1)} custom-call(s32[128]{0:T(128)S(1)} %reshape.8.shift_ref, bf16[512,2048]{1,0:T(8,128)(2,1)S(1)} %bitcast.12, bf16[16,2048]{1,0:T(8,128)(2,1)S(1)} %collective-permute-done.before_ref, bf16[16,2048]{1,0:T(8,128)(2,1)S(1)} %collective-permute-done.1.after_ref), custom_call_target="tpu_custom_call" | custom-call | tf_op jit(solution)/shard_map/register/pallas_call | solution.py:75
  12.9 0.0 copy-done.2
  12.9 0.0 copy-done.3
  12.9 0.0 copy-done.4
  12.9 52.0 %exchange_project.1 = f32[256,128]{1,0:T(8,128)S(1)} custom-call(bf16[8,64,2048]{2,1,0:T(8,128)(2,1)S(1)} %bitcast.11, bf16[32,64,4096]{2,1,0:T(8,128)(2,1)} %bitcast.14, s32[8,1,256]{2,1,0:T(1,128)S(1)} %reshape_squeeze.3.refs_2_, bf16[256,256]{1,0:T(8,128)(2,1)S(1)} %copy-done.3, bf16[256,256]{1,0:T(8,128)(2,1)S(1)} %copy-done.4, ...), custom_call_target="tpu_custom_call" | custom-call | tf_op jit(solution)/shard_map/exchange_project/pallas_call | solution.py:277
  64.9 0.0 copy-start.1
  64.9 0.6 copy-done.1
  65.5 12.4 %collect.1 = f32[8,128]{1,0:T(8,128)} custom-call(f32[32,8,128]{2,1,0:T(8,128)} %bitcast.13), custom_call_target="tpu_custom_call" | custom-call | tf_op jit(solution)/shard_map/collect/pallas_call | solution.py:245
  77.9 1.3 %copy.11 = f32[128,8]{0,1:T(8,128)} copy(f32[128,8]{0,1:T(8,128)} %bitcast.15) | data formatting | bytes 8192
Async XLA Ops:
  0.9 5.4 %collective-permute-start = (bf16[16,2048]{1,0:T(8,128)(2,1)S(1)}, bf16[16,2048]{1,0:T(8,128)(2,1)S(1)}, u32[]{:S(2)}, u32[]{:S(2)}) collective-permute-start(bf16[16,2048]{1,0:T(8,128)(2,1)S(1)} %get-tuple-element.6), channel_id=1, source_target_pairs={{0,1},{1,2},{2,3},{4,5},{5,6},{6,7},{8,9},{9,10},{10,11},{12,13},{... | collective-permute-start | bytes 196616 | tf_op jit(solution)/shard_map/ppermute | solution.py:34
  3.3 5.3 %collective-permute-start.1 = (bf16[16,2048]{1,0:T(8,128)(2,1)S(1)}, bf16[16,2048]{1,0:T(8,128)(2,1)S(1)}, u32[]{:S(2)}, u32[]{:S(2)}) collective-permute-start(bf16[16,2048]{1,0:T(8,128)(2,1)S(1)} %get-tuple-element.5), channel_id=1, source_target_pairs={{1,0},{2,1},{3,2},{5,4},{6,5},{7,6},{9,8},{10,9},{11,10},{13,12},{... | collective-permute-start | bytes 196616 | tf_op jit(solution)/shard_map/ppermute | solution.py:35
  8.5 1.6 %copy-start = (bf16[1,512,2048]{2,1,0:T(8,128)(2,1)S(1)}, bf16[1,512,2048]{2,1,0:T(8,128)(2,1)}, u32[]{:S(2)}) copy-start(bf16[1,512,2048]{2,1,0:T(8,128)(2,1)} %param.7) | copy-start | bytes 6291460
  10.1 2.7 %copy-start.2 = (bf16[256,512]{1,0:T(8,128)(2,1)S(1)}, bf16[256,512]{1,0:T(8,128)(2,1)}, u32[]{:S(2)}) copy-start(bf16[256,512]{1,0:T(8,128)(2,1)} %constant.8.clone.refs_5_) | copy-start | bytes 786436
  10.1 2.7 %copy-start.3 = (bf16[256,256]{1,0:T(8,128)(2,1)S(1)}, bf16[256,256]{1,0:T(8,128)(2,1)}, u32[]{:S(2)}) copy-start(bf16[256,256]{1,0:T(8,128)(2,1)} %constant.6.clone.refs_3_) | copy-start | bytes 393220
  10.1 2.8 %copy-start.4 = (bf16[256,256]{1,0:T(8,128)(2,1)S(1)}, bf16[256,256]{1,0:T(8,128)(2,1)}, u32[]{:S(2)}) copy-start(bf16[256,256]{1,0:T(8,128)(2,1)} %constant.7.clone.refs_4_) | copy-start | bytes 393220
  64.9 0.7 copy-start.1
